TPU v7x, 32 devices: a whole 2x2x4 slice. The times are simulated.
32 devices in a mesh: row: 4 (over y, core), col: 8 (over z, x).
Axes of the slice: x: 2, y: 2, z: 4, core: 2. Of those that a mesh axis runs over, the one named last changes fastest.
Arguments:
- amplitudes: float32 [1024, 1024], P('row', 'col'), may hold values from -8 to 8, as said below
- factors: float32 [1024, 1536], P(('row', 'col')), may hold values from -1.5 to 1.5
- occ_map: int32 [1024], P(('row', 'col')), may hold values from 0 to 127
- vir_map: int32 [1024], P(('row', 'col')), may hold values from 0 to 1023
- occ_energy: float32 [128], replicated, may hold values from -2 to -0.3
- vir_energy: float32 [1024], replicated, may hold values from 0.2 to 3
Outputs:
- new_amplitudes: float32 [1024, 1024], P('row', 'col')
- density: float32 [1024, 1536], P('row', 'col')
Inputs may be any that keep to these rules, and one draw needn't show every extreme that they name: amplitudes equals its transpose, up to float32 rounding.
All inputs are finite; a program needn't handle non-finite values.
Results may differ from a plain program's by a relative error of at most 0.00012.
Values sent between devices are 32-bit elements; how exact they have to be, the bound alone decides.
A program may use at most 64 MiB of HBM per device.

v0:
```python
import functools

import jax
import jax.numpy as jnp
from jax import lax
from jax.experimental import pallas as pl
from jax.experimental.pallas import tpu as pltpu
from jax.sharding import PartitionSpec as P

HIGHEST = lax.Precision.HIGHEST
MESH = pl.DeviceIdType.MESH
LANES = 128
SUB = 8


def spread(x, axis, root):
    mine = lax.axis_index(axis) == root
    return lax.psum(jnp.where(mine, x, jnp.zeros_like(x)), axis)


def pair_energies(occ_map, vir_map, occ_energy, vir_energy):
    def pick(index, table):
        hot = index[:, None] == jnp.arange(table.shape[0], dtype=jnp.int32)[None, :]
        return jnp.sum(jnp.where(hot, table[None, :], 0.0), axis=1)

    return pick(vir_map, vir_energy) - pick(occ_map, occ_energy)


def general(amplitudes, factors, occ_map, vir_map, occ_energy, vir_energy):
    col_ratio = lax.axis_size("col") // lax.axis_size("row")
    column = lax.axis_index("col")
    pair_energy = pair_energies(occ_map, vir_map, occ_energy, vir_energy)
    row_factor, row_energy = (
        lax.all_gather(factors, "col", axis=0, tiled=True),
        lax.all_gather(pair_energy, "col", axis=0, tiled=True),
    )
    tile_width = amplitudes.shape[1]
    offset = column % col_ratio * tile_width
    source = column // col_ratio
    col_factor, col_energy = (
        spread(lax.dynamic_slice_in_dim(row_factor, offset, tile_width, 0), "row", source),
        spread(lax.dynamic_slice_in_dim(row_energy, offset, tile_width, 0), "row", source),
    )
    mixed_rows = lax.psum(
        jnp.dot(amplitudes, col_factor, precision=HIGHEST, preferred_element_type=jnp.float32),
        "col",
    )
    transposed = lax.dot_general(
        amplitudes,
        row_factor,
        (((0,), (0,)), ((), ())),
        precision=HIGHEST,
        preferred_element_type=jnp.float32,
    )
    mixed_cols = lax.psum(transposed, "row")
    contract = (((1,), (1,)), ((), ()))
    residual = lax.dot_general(
        row_factor + mixed_rows,
        col_factor,
        contract,
        precision=HIGHEST,
        preferred_element_type=jnp.float32,
    )
    residual = residual + lax.dot_general(
        row_factor, mixed_cols, contract, precision=HIGHEST, preferred_element_type=jnp.float32
    )
    new_amp = -residual / (row_energy[:, None] + col_energy[None, :])
    dens_terms = jnp.dot(new_amp, col_factor, precision=HIGHEST, preferred_element_type=jnp.float32)
    density = lax.psum_scatter(dens_terms, "col", scatter_dimension=1, tiled=True)
    return (new_amp, density)


def halves(v):
    high = v.astype(jnp.bfloat16)
    return high, (v - high.astype(jnp.float32)).astype(jnp.bfloat16)


def dot3(a, b, dims):
    (ah, al), (bh, bl) = a, b
    dot = functools.partial(
        lax.dot_general, dimension_numbers=(dims, ((), ())), preferred_element_type=jnp.float32
    )
    return dot(ah, bh) + (dot(ah, bl) + dot(al, bh))


NN = ((1,), (0,))
NT = ((1,), (1,))


def kernel(
    n_row, ratio, own, width,
    f_ref, a_ref, om_ref, vm_ref, oe_ref, ve_ref, t_ref, o_ref,
    fp, pv, pb, fb, fh, fl, ab, sp, sr1, sp2, sr2, st, xr, tb, mx, db,
    f1s, f1r, pvs, pvr, zs, zr, as_, ar, ps, pr, s1s, s1r, s2s, s2r, xs, xrs,
    ts, tr, us, ur, ds_, dr,
):
    n_z = n_row
    r = lax.axis_index("row")
    c = lax.axis_index("col")
    z, x = c // ratio, c % ratio
    k = r % 2
    h = r // 2
    mate = r + 1 - 2 * k
    n_h = n_row // 2
    rows, cols = a_ref.shape
    half = own // 2
    rest = width - LANES
    me = r * ratio + x

    def copy(src, dst, send, recv, row, col):
        return pltpu.make_async_remote_copy(
            src_ref=src, dst_ref=dst, send_sem=send, recv_sem=recv,
            device_id=(row, col), device_id_type=MESH,
        )

    def arrived(buf, recv):
        copy(buf, buf, ds_.at[0], recv, mate, c).wait_recv()

    def greet(row, col):
        pl.semaphore_signal(
            pltpu.get_barrier_semaphore(), inc=1, device_id=(row, col), device_id_type=MESH
        )

    def place(dh, dx, dk):
        return ((h + dh) % n_h) * 2 + (k + dk) % 2, (x + dx) % ratio

    group8 = [(dh, dx, dk) for dh in range(n_h) for dx in range(ratio) for dk in range(2)]
    plane = group8[1:]
    peers = [(dh, dx) for dh in range(n_h) for dx in range(ratio) if dh or dx]

    for off in plane:
        row, xx = place(*off)
        greet(row, z * ratio + xx)

    @pl.when(z > 0)
    def _():
        greet(r, c - ratio)

    @pl.when(z < n_z - 1)
    def _():
        greet(r, c + ratio)

    for p in range(n_row * ratio):
        fp[p, :own] = f_ref[:, p * width:p * width + LANES]
        tail = f_ref[:, p * width + LANES:(p + 1) * width]
        fp[p, own:] = jnp.concatenate([tail[:half], tail[half:]], axis=1)
    fb[r, z, x] = fp[me]

    def pick(index_ref, table_ref):
        size = table_ref.shape[1]
        index = jnp.broadcast_to(index_ref[...].astype(jnp.float32), (own, own))
        diag = lax.broadcasted_iota(jnp.int32, (own, own), 0) == lax.broadcasted_iota(jnp.int32, (own, own), 1)
        column = jnp.sum(jnp.where(diag, index, 0.0), axis=1, keepdims=True)
        spot = lax.broadcasted_iota(jnp.int32, (own, size), 1).astype(jnp.float32)
        table = jnp.broadcast_to(table_ref[...], (own, size))
        return jnp.sum(jnp.where(spot == column, table, 0.0), axis=1, keepdims=True)

    pe = pick(vm_ref, ve_ref) - pick(om_ref, oe_ref)
    turn = lax.broadcasted_iota(jnp.int32, (own, LANES), 0) == lax.broadcasted_iota(jnp.int32, (own, LANES), 1) % own
    pe_row = jnp.sum(jnp.where(turn, jnp.broadcast_to(pe, (own, LANES)), 0.0), axis=0, keepdims=True)
    pv[me] = jnp.broadcast_to(pe_row, (SUB, LANES))
    ab[r, x] = a_ref[...].T
    expect = len(plane) + jnp.where(z > 0, 1, 0) + jnp.where(z < n_z - 1, 1, 0)
    pl.semaphore_wait(pltpu.get_barrier_semaphore(), expect)

    pending = []

    def piece(b, off):
        if off is None:
            return pb.at[b], n_row * ratio
        row, xx = place(*off)
        return fb.at[row, b, xx], row * ratio + xx

    def hops(s, off):
        def right():
            buf, i = piece(z - s, off)
            return copy(buf, buf, zs.at[0, s, i], zr.at[z - s, i], r, c + ratio)

        def left():
            buf, i = piece(z + s, off)
            return copy(buf, buf, zs.at[1, s, i], zr.at[z + s, i], r, c - ratio)

        return ((z < n_z - 1) & (z >= s), right), ((z > 0) & (z + s < n_z), left)

    def line_send(s, off):
        for go, make in hops(s, off):
            @pl.when(go)
            def _(make=make):
                make().start()

    def line_step(s, off):
        for there, b, (go, make) in zip(((z >= s), (z + s < n_z)), (z - s, z + s), hops(s, off)):
            @pl.when(there)
            def _(b=b):
                buf, i = piece(b, off)
                arrived(buf, zr.at[b, i])

            if s < n_z - 1:
                @pl.when(go)
                def _(make=make):
                    make().start()

    line_send(0, group8[0])
    for i, off in enumerate(plane):
        row, xx = place(*off)
        cp = copy(fp.at[row * ratio + xx], fb.at[r, z, x], f1s.at[i], f1r.at[me], row, z * ratio + xx)
        cp.start()
        pending.append(cp)
    for i, off in enumerate(plane):
        row, xx = place(*off)
        cp = copy(pv.at[me], pv.at[me], pvs.at[i], pvr.at[me], row, z * ratio + xx)
        cp.start()
        pending.append(cp)

    def gather_start(buf, at, send, recv, mate_send, mate_recv):
        for i, (dh, dx) in enumerate(peers):
            row, xx = place(dh, dx, 0)
            cp = copy(buf.at[r, x, at], buf.at[r, x, at], send.at[at, i], recv.at[at, h, x], row, z * ratio + xx)
            cp.start()
            pending.append(cp)
        cp = copy(
            buf.at[r, x, at], buf.at[r, x, at], mate_send.at[at, len(peers)], mate_recv.at[at, h, x], mate, c
        )
        cp.start()
        pending.append(cp)

    def gather_relay(buf, at, recv, mate_send, mate_recv):
        for i, (dh, dx) in enumerate(peers):
            row, xx = place(dh, dx, 0)
            hh = row // 2
            arrived(buf.at[row, xx, at], recv.at[at, hh, xx])
            cp = copy(buf.at[row, xx, at], buf.at[row, xx, at], mate_send.at[at, i], mate_recv.at[at, hh, xx], mate, c)
            cp.start()
            pending.append(cp)

    def gather_end(buf, at, mate_recv):
        for hh in range(n_h):
            for xx in range(ratio):
                arrived(buf.at[hh * 2 + 1 - k, xx, at], mate_recv.at[at, hh, xx])

    for i, (dh, dx) in enumerate(peers):
        row, xx = place(dh, dx, 0)
        cp = copy(ab.at[r, x], ab.at[r, x], as_.at[i], ar.at[h, x], row, z * ratio + xx)
        cp.start()
        pending.append(cp)
    cp = copy(ab.at[r, x], ab.at[r, x], ps.at[len(peers)], pr.at[h, x], mate, c)
    cp.start()
    pending.append(cp)
    for off in plane:
        row, xx = place(*off)
        arrived(fb.at[row, z, xx], f1r.at[row * ratio + xx])
        line_send(0, off)
    sub = lax.broadcasted_iota(jnp.int32, (SUB, LANES), 0)
    marks = jnp.where(sub == me, pv[me], 0.0)
    for off in plane:
        row, xx = place(*off)
        i = row * ratio + xx
        arrived(pv.at[i], pvr.at[i])
        marks = jnp.where(sub == i, pv[i], marks)
    pb[z] = marks
    for off in group8:
        line_step(1, off)
    def relay_tiles():
        for i, (dh, dx) in enumerate(peers):
            row, xx = place(dh, dx, 0)
            hh = row // 2
            arrived(ab.at[row, xx], ar.at[hh, xx])
            cp = copy(ab.at[row, xx], ab.at[row, xx], ps.at[i], pr.at[hh, xx], mate, c)
            cp.start()
            pending.append(cp)

    line_send(0, None)
    for s in range(2, n_z):
        for off in group8:
            line_step(s, off)
        if s == 2:
            line_step(1, None)
            relay_tiles()
    for s in range(2, n_z):
        line_step(s, None)
    for hh in range(n_h):
        for xx in range(ratio):
            arrived(ab.at[hh * 2 + 1 - k, xx], pr.at[hh, xx])
    for rr in range(n_row):
        for b in range(n_z):
            for xx in range(ratio):
                top = (b * ratio + xx) * own
                ph, plo = halves(fb[rr, b, xx])
                for ref, val in ((fh, ph), (fl, plo)):
                    ref[rr, top:top + own, :LANES] = val[:own]
                    ref[rr, top:top + half, LANES:] = val[own:, :rest]
                    ref[rr, top + half:top + own, LANES:] = val[own:, rest:]

    def fac(rr):
        return fh[rr], fl[rr]

    for xx in range(ratio):
        m = fh[z, xx * cols:(xx + 1) * cols].astype(jnp.float32)
        m = 0.5 * (m + fl[z, xx * cols:(xx + 1) * cols].astype(jnp.float32))
        for rr in range(n_row):
            m = m + dot3(halves(ab[rr, xx]), fac(rr), NN)
        mx[xx] = m
    left_side = [[v for v in halves(mx[xx])] for xx in range(ratio)]
    left_all = tuple(jnp.concatenate([left_side[xx][i] for xx in range(ratio)], axis=0) for i in range(2))

    order = [n_h - 1 - j for j in range(n_h)]
    for dh in order:
        row = ((h + dh) % n_h) * 2 + 1 - k
        hh = row // 2
        both = dot3(fac(row), left_all, NT)
        for xx in range(ratio):
            sp[row, xx] = both[:, xx * cols:(xx + 1) * cols]
            cp = copy(sp.at[row, xx], sr1.at[hh, xx], s1s.at[hh, xx], s1r.at[hh, xx], mate, c)
            cp.start()
            pending.append(cp)
    for dh in order:
        row = ((h + dh) % n_h) * 2 + k
        both = dot3(fac(row), left_all, NT)
        for xx in range(ratio):
            sp[row, xx] = both[:, xx * cols:(xx + 1) * cols]
    for i, (dh, dx) in enumerate(reversed(peers)):
        row, xx = place(dh, dx, 0)
        hh = row // 2
        arrived(sr1.at[hh, xx], s1r.at[hh, xx])
        sp2[hh, xx] = sp[row, xx] + sr1[hh, xx]
        cp = copy(sp2.at[hh, xx], sr2.at[h, x], s2s.at[i], s2r.at[h, x], row, z * ratio + xx)
        cp.start()
        pending.append(cp)
    arrived(sr1.at[h, x], s1r.at[h, x])
    total = sp[r, x] + sr1[h, x]
    for dh, dx in peers:
        row, xx = place(dh, dx, 0)
        hh = row // 2
        arrived(sr2.at[hh, xx], s2r.at[hh, xx])
        total = total + sr2[hh, xx]
    st[...] = total
    def swap(xx):
        return copy(st.at[pl.ds(xx * cols, cols)], xr.at[x], xs.at[xx], xrs.at[x], z, r * ratio + xx)

    for xx in range(ratio):
        @pl.when((r != z) | (x != xx))
        def _(xx=xx):
            swap(xx).start()

    @pl.when(r == z)
    def _():
        xr[x] = st[pl.ds(pl.multiple_of(x * cols, cols), cols)]

    lane = lax.broadcasted_iota(jnp.int32, (1, LANES), 1)
    group = LANES // own

    def energy(rr, first):
        out = jnp.zeros((1, LANES), jnp.float32)
        for j in range(group):
            at = first + j
            row = pb[at // ratio, pl.ds(rr * ratio + at % ratio, 1)]
            out = jnp.where(lane // own == j, row, out)
        return jnp.broadcast_to(out, (LANES, LANES))

    col_energy = energy(z, x * group)
    row_energy = [energy(r, xx * group).T for xx in range(ratio)]

    for xx in range(ratio):
        @pl.when((r != z) | (x != xx))
        def _(xx=xx):
            arrived(xr.at[xx], xrs.at[xx])

        part = slice(xx * cols, (xx + 1) * cols)
        new = -(st[part] + xr[xx].T) / (row_energy[xx] + col_energy)
        tb[r, x, xx] = new.T
        gather_start(tb, xx, ts, tr, us, ur)
        t_ref[part] = new

    for xx in range(ratio):
        gather_relay(tb, xx, tr, us, ur)
    for xx in range(ratio):
        gather_end(tb, xx, ur)

    def home(xx):
        part = pl.ds(xx * cols, cols)
        return copy(db.at[:, part], o_ref.at[:, part], ds_.at[xx], dr.at[xx], z, r * ratio + x)

    for xx in range(ratio):
        d = None
        for rr in range(n_row):
            tile = jnp.concatenate([tb[rr, xx, i] for i in range(ratio)], axis=1)
            term = dot3(halves(tile), fac(rr), NN)
            d = term if d is None else d + term
        part = slice(xx * cols, (xx + 1) * cols)
        db[:LANES, part] = d[:, :LANES].T
        db[LANES:, part] = d[:, LANES:].T

        @pl.when(r != z)
        def _(xx=xx):
            home(xx).start()

    @pl.when(r == z)
    def _():
        o_ref[...] = db[...]

    for cp in pending:
        cp.wait_send()
    for s in range(n_z - 1):
        for off in group8 + [None]:
            for go, make in hops(s, off):
                @pl.when(go)
                def _(make=make):
                    make().wait_send()
    for xx in range(ratio):
        @pl.when((r != z) | (x != xx))
        def _(xx=xx):
            swap(xx).wait_send()

    @pl.when(r != z)
    def _():
        for xx in range(ratio):
            home(xx).wait_send()
            home(xx).wait_recv()


def settle(new_ref, turned_ref, new_out, turned_out):
    new_out[...] = new_ref[...]
    turned_out[...] = turned_ref[...]


def fits(mesh, rows, cols, own, width):
    n_row, n_col = mesh.shape["row"], mesh.shape["col"]
    ratio = n_col // n_row
    return (
        n_col == ratio * n_row and n_col == SUB and ratio == 2 and n_row % 2 == 0
        and rows == ratio * cols and cols == LANES
        and rows == n_col * own and LANES % own == 0 and own % (4 * SUB) == 0
        and 2 * width == 3 * LANES and 60 * rows * rows * n_row <= 64 * 2**20
    )


def fused(n_row, ratio, amplitudes, factors, occ_map, vir_map, occ_energy, vir_energy):
    rows, cols = amplitudes.shape
    own, n_aux = factors.shape
    n_col = n_row * ratio
    width = n_aux // n_col
    n_h = n_row // 2
    peers = n_h * ratio - 1
    deep = own + own // 2
    f32, bf16 = jnp.float32, jnp.bfloat16
    dma = pltpu.SemaphoreType.DMA
    vmem = pl.BlockSpec(memory_space=pltpu.VMEM)
    new, turned = pl.pallas_call(
        functools.partial(kernel, n_row, ratio, own, width),
        out_shape=(
            jax.ShapeDtypeStruct((rows, cols), f32),
            jax.ShapeDtypeStruct((width, rows), f32),
        ),
        in_specs=[vmem] * 6,
        out_specs=(vmem, vmem),
        scratch_shapes=[
            pltpu.VMEM((n_col, deep, LANES), f32),
            pltpu.VMEM((n_col, SUB, LANES), f32),
            pltpu.VMEM((n_row, SUB, LANES), f32),
            pltpu.VMEM((n_row, n_row, ratio, deep, LANES), f32),
            pltpu.VMEM((n_row, rows, width), bf16),
            pltpu.VMEM((n_row, rows, width), bf16),
            pltpu.VMEM((n_row, ratio, cols, rows), f32),
            pltpu.VMEM((n_row, ratio, rows, cols), f32),
            pltpu.VMEM((n_h, ratio, rows, cols), f32),
            pltpu.VMEM((n_h, ratio, rows, cols), f32),
            pltpu.VMEM((n_h, ratio, rows, cols), f32),
            pltpu.VMEM((rows, cols), f32),
            pltpu.VMEM((ratio, cols, cols), f32),
            pltpu.VMEM((n_row, ratio, ratio, cols, cols), f32),
            pltpu.VMEM((ratio, cols, width), f32),
            pltpu.VMEM((width, rows), f32),
            dma((n_col - 1,)), dma((n_col,)),
            dma((n_col - 1,)), dma((n_col,)),
            dma((2, n_row, n_col + 1)), dma((n_row, n_col + 1)),
            dma((peers,)), dma((n_h, ratio)),
            dma((peers + 1,)), dma((n_h, ratio)),
            dma((n_h, ratio)), dma((n_h, ratio)),
            dma((peers,)), dma((n_h, ratio)),
            dma((ratio,)), dma((ratio,)),
            dma((ratio, peers)), dma((ratio, n_h, ratio)),
            dma((ratio, peers + 1)), dma((ratio, n_h, ratio)),
            dma((ratio,)), dma((ratio,)),
        ],
        compiler_params=pltpu.CompilerParams(collective_id=0, has_side_effects=True),
    )(
        factors, amplitudes, occ_map[None, :], vir_map[None, :], occ_energy[None, :], vir_energy[None, :]
    )
    new, turned = pl.pallas_call(
        settle,
        out_shape=(
            jax.ShapeDtypeStruct((rows, cols), f32),
            jax.ShapeDtypeStruct((width, rows), f32),
        ),
        in_specs=[vmem, vmem],
        out_specs=(vmem, vmem),
    )(new, turned)
    return new, turned.T


def solution(mesh):
    n_row, n_col = mesh.shape["row"], mesh.shape["col"]

    def per_device(amplitudes, factors, *rest):
        rows, cols = amplitudes.shape
        own, n_aux = factors.shape
        if fits(mesh, rows, cols, own, n_aux // n_col):
            return fused(n_row, n_col // n_row, amplitudes, factors, *rest)
        return general(amplitudes, factors, *rest)

    placed = (
        P("row", "col"),
        P(("row", "col"), None),
        P(("row", "col")),
        P(("row", "col")),
        P(),
        P(),
    )
    return jax.shard_map(
        per_device,
        mesh=mesh,
        in_specs=placed,
        out_specs=(P("row", "col"), P("row", "col")),
        check_vma=False,
    )
```

profile of v0, /device:TPU:4, one launch (start us, length us, event | category | flops | bytes accessed | tf_op | source)
XLA Modules:
  0.0 59.9 jit_solution(3767382147686198991)
XLA Ops:
  0.6 57.6 %shard_map.77 = (f32[256,128]{1,0:T(8,128)}, f32[192,256]{1,0:T(8,128)}) custom-call(f32[32,1536]{1,0:T(8,128)} %f_ref.1, f32[256,128]{1,0:T(8,128)} %a_ref.1, s32[1,32]{1,0:T(1,128)} %bitcast.6, s32[1,32]{1,0:T(1,128)} %bitcast.7, f32[1,128]{1,0:T(1,128)} %bitcast.8, f32[1,1024]{1,0:T(1,128)} %bitcast.5), custom_call_target="tpu_custom_call" | custom-call | tf_op jit(solution)/shard_map/pallas_call | solution.py:448
  58.2 1.7 %shard_map.78 = (f32[256,128]{1,0:T(8,128)}, f32[192,256]{1,0:T(8,128)}) custom-call(f32[256,128]{1,0:T(8,128)} %get-tuple-element.6.new_ref, f32[192,256]{1,0:T(8,128)} %get-tuple-element.7.turned_ref), custom_call_target="tpu_custom_call" | custom-call | tf_op jit(solution)/shard_map/pallas_call | solution.py:489
where the time goes:
time: 60.1 us; the launch traced here: 59.9 us
  Pallas kernels  59.3 us (99%)
  between operations  0.64 us (1%)
    pallas_call x1, Pallas kernels, fused(): pl.pallas_call(functools.partial(kernel, n_row, ratio, own, width), out_s...  57.6 us
    pallas_call x1, Pallas kernels, fused(): pl.pallas_call(settle, out_shape=(jax.ShapeDtypeStruct((rows, cols), f32)...  1.72 us

commit v1 on v0

--- a/solution.py
+++ b/solution.py
@@ -107,6 +107,12 @@
     rest = width - LANES
     me = r * ratio + x
 
+    def part_of(row):
+        return (row % 2) * n_h + row // 2
+
+    goal = part_of(r)
+    stays = (r == z) & (goal == z)
+
     def copy(src, dst, send, recv, row, col):
         return pltpu.make_async_remote_copy(
             src_ref=src, dst_ref=dst, send_sem=send, recv_sem=recv,
@@ -144,7 +150,7 @@
         fp[p, :own] = f_ref[:, p * width:p * width + LANES]
         tail = f_ref[:, p * width + LANES:(p + 1) * width]
         fp[p, own:] = jnp.concatenate([tail[:half], tail[half:]], axis=1)
-    fb[r, z, x] = fp[me]
+    fb[r, z, x] = fp[goal * ratio + x]
 
     def pick(index_ref, table_ref):
         size = table_ref.shape[1]
@@ -203,7 +209,7 @@
     line_send(0, group8[0])
     for i, off in enumerate(plane):
         row, xx = place(*off)
-        cp = copy(fp.at[row * ratio + xx], fb.at[r, z, x], f1s.at[i], f1r.at[me], row, z * ratio + xx)
+        cp = copy(fp.at[part_of(row) * ratio + xx], fb.at[r, z, x], f1s.at[i], f1r.at[me], row, z * ratio + xx)
         cp.start()
         pending.append(cp)
     for i, off in enumerate(plane):
@@ -378,7 +384,7 @@
 
     def home(xx):
         part = pl.ds(xx * cols, cols)
-        return copy(db.at[:, part], o_ref.at[:, part], ds_.at[xx], dr.at[xx], z, r * ratio + x)
+        return copy(db.at[:, part], o_ref.at[:, part], ds_.at[xx], dr.at[xx], z, goal * ratio + x)
 
     for xx in range(ratio):
         d = None
@@ -390,11 +396,11 @@
         db[:LANES, part] = d[:, :LANES].T
         db[LANES:, part] = d[:, LANES:].T
 
-        @pl.when(r != z)
+        @pl.when(~stays)
         def _(xx=xx):
             home(xx).start()
 
-    @pl.when(r == z)
+    @pl.when(stays)
     def _():
         o_ref[...] = db[...]
 
@@ -411,7 +417,7 @@
         def _(xx=xx):
             swap(xx).wait_send()
 
-    @pl.when(r != z)
+    @pl.when(~stays)
     def _():
         for xx in range(ratio):
             home(xx).wait_send()

time: 60.1 us -> 59.3 us (0.987)
  the two profiles are of different devices: /device:TPU:4 before, /device:TPU:1 now
where the time goes in v1:
time: 59.3 us; the launch traced here: 59.1 us
  Pallas kernels  58.5 us (99%)
  between operations  0.64 us (1%)
    pallas_call x1, Pallas kernels, fused(): pl.pallas_call(functools.partial(kernel, n_row, ratio, own, width), out_s...  56.8 us
    pallas_call x1, Pallas kernels, fused(): pl.pallas_call(settle, out_shape=(jax.ShapeDtypeStruct((rows, cols), f32)...  1.72 us

profile of v1, /device:TPU:1, one launch (start us, length us, event | category | flops | bytes accessed | tf_op | source)
XLA Modules:
  0.0 59.1 jit_solution(8759742282362509280)
XLA Ops:
  0.6 56.8 %shard_map.77 = (f32[256,128]{1,0:T(8,128)}, f32[192,256]{1,0:T(8,128)}) custom-call(f32[32,1536]{1,0:T(8,128)} %f_ref.1, f32[256,128]{1,0:T(8,128)} %a_ref.1, s32[1,32]{1,0:T(1,128)} %bitcast.6, s32[1,32]{1,0:T(1,128)} %bitcast.7, f32[1,128]{1,0:T(1,128)} %bitcast.8, f32[1,1024]{1,0:T(1,128)} %bitcast.5), custom_call_target="tpu_custom_call" | custom-call | tf_op jit(solution)/shard_map/pallas_call | solution.py:454
  57.4 1.7 %shard_map.78 = (f32[256,128]{1,0:T(8,128)}, f32[192,256]{1,0:T(8,128)}) custom-call(f32[256,128]{1,0:T(8,128)} %get-tuple-element.6.new_ref, f32[192,256]{1,0:T(8,128)} %get-tuple-element.7.turned_ref), custom_call_target="tpu_custom_call" | custom-call | tf_op jit(solution)/shard_map/pallas_call | solution.py:495

commit v2 on v1

--- a/solution.py
+++ b/solution.py
@@ -89,9 +89,10 @@
 
 def kernel(
     n_row, ratio, own, width,
-    f_ref, a_ref, om_ref, vm_ref, oe_ref, ve_ref, t_ref, o_ref,
-    fp, pv, pb, fb, fh, fl, ab, sp, sr1, sp2, sr2, st, xr, tb, mx, db,
-    f1s, f1r, pvs, pvr, zs, zr, as_, ar, ps, pr, s1s, s1r, s2s, s2r, xs, xrs,
+    f_hbm, a_hbm, om_hbm, vm_hbm, oe_hbm, ve_hbm, t_ref, o_ref,
+    f_ref, a_ref, om_ref, vm_ref, oe_ref, ve_ref,
+    fp, pv, pb, fb, fh, fl, ab, sp, so, sr, ax, axr, ay, ayr, bx, bxr, by, byr, st, xr, tb, mx, db,
+    ld, f1s, f1r, pvs, pvr, zs, zr, as_, ar, ps, pr, ms, mr, rs, rr_, xs, xrs,
     ts, tr, us, ur, ds_, dr,
 ):
     n_z = n_row
@@ -101,8 +102,11 @@
     k = r % 2
     h = r // 2
     mate = r + 1 - 2 * k
+    near_x = (r, z * ratio + 1 - x)
+    near_y = ((1 - r // 2) * 2 + k, c)
     n_h = n_row // 2
     rows, cols = a_ref.shape
+    fine = cols // 2
     half = own // 2
     rest = width - LANES
     me = r * ratio + x
@@ -146,6 +150,15 @@
     def _():
         greet(r, c + ratio)
 
+    loads = [
+        pltpu.make_async_copy(src, dst, ld.at[i])
+        for i, (src, dst) in enumerate((
+            (f_hbm, f_ref), (a_hbm, a_ref), (om_hbm, om_ref), (vm_hbm, vm_ref), (oe_hbm, oe_ref), (ve_hbm, ve_ref)
+        ))
+    ]
+    for load in loads:
+        load.start()
+    loads[0].wait()
     for p in range(n_row * ratio):
         fp[p, :own] = f_ref[:, p * width:p * width + LANES]
         tail = f_ref[:, p * width + LANES:(p + 1) * width]
@@ -161,6 +174,8 @@
         table = jnp.broadcast_to(table_ref[...], (own, size))
         return jnp.sum(jnp.where(spot == column, table, 0.0), axis=1, keepdims=True)
 
+    for load in loads[1:]:
+        load.wait()
     pe = pick(vm_ref, ve_ref) - pick(om_ref, oe_ref)
     turn = lax.broadcasted_iota(jnp.int32, (own, LANES), 0) == lax.broadcasted_iota(jnp.int32, (own, LANES), 1) % own
     pe_row = jnp.sum(jnp.where(turn, jnp.broadcast_to(pe, (own, LANES)), 0.0), axis=0, keepdims=True)
@@ -218,31 +233,10 @@
         cp.start()
         pending.append(cp)
 
-    def gather_start(buf, at, send, recv, mate_send, mate_recv):
-        for i, (dh, dx) in enumerate(peers):
-            row, xx = place(dh, dx, 0)
-            cp = copy(buf.at[r, x, at], buf.at[r, x, at], send.at[at, i], recv.at[at, h, x], row, z * ratio + xx)
-            cp.start()
-            pending.append(cp)
-        cp = copy(
-            buf.at[r, x, at], buf.at[r, x, at], mate_send.at[at, len(peers)], mate_recv.at[at, h, x], mate, c
-        )
+    def send(src, dst, out, into, row, col):
+        cp = copy(src, dst, out, into, row, col)
         cp.start()
         pending.append(cp)
-
-    def gather_relay(buf, at, recv, mate_send, mate_recv):
-        for i, (dh, dx) in enumerate(peers):
-            row, xx = place(dh, dx, 0)
-            hh = row // 2
-            arrived(buf.at[row, xx, at], recv.at[at, hh, xx])
-            cp = copy(buf.at[row, xx, at], buf.at[row, xx, at], mate_send.at[at, i], mate_recv.at[at, hh, xx], mate, c)
-            cp.start()
-            pending.append(cp)
-
-    def gather_end(buf, at, mate_recv):
-        for hh in range(n_h):
-            for xx in range(ratio):
-                arrived(buf.at[hh * 2 + 1 - k, xx, at], mate_recv.at[at, hh, xx])
 
     for i, (dh, dx) in enumerate(peers):
         row, xx = place(dh, dx, 0)
@@ -309,48 +303,63 @@
     left_side = [[v for v in halves(mx[xx])] for xx in range(ratio)]
     left_all = tuple(jnp.concatenate([left_side[xx][i] for xx in range(ratio)], axis=0) for i in range(2))
 
-    order = [n_h - 1 - j for j in range(n_h)]
-    for dh in order:
-        row = ((h + dh) % n_h) * 2 + 1 - k
-        hh = row // 2
-        both = dot3(fac(row), left_all, NT)
+    def strip(row, q):
+        parts = [slice(j * cols + q * fine, j * cols + (q + 1) * fine) for j in range(ratio)]
+        return tuple(jnp.concatenate([ref[row, part] for part in parts], axis=0) for ref in (fh, fl))
+
+    def products(ref, q, yy, row):
+        both = dot3(strip(row, q), left_all, NT)
+        for j in range(ratio):
+            for xx in range(ratio):
+                ref[q, yy, j, xx] = both[j * fine:(j + 1) * fine, xx * cols:(xx + 1) * cols]
+
+    for q in range(2):
+        for yy in range(n_h):
+            products(sp, q, yy, yy * 2 + 1 - k)
+        send(sp.at[q], sr.at[q], ms.at[q], mr.at[q], mate, c)
+    for q in range(2):
+        for yy in range(n_h):
+            products(so, q, yy, yy * 2 + k)
+
+    def pair(q, yy, j, xx):
+        return so[q, yy, j, xx] + sr[q, yy, j, xx]
+
+    for q in range(2):
+        arrived(sr.at[q], mr.at[q])
+        for yy in range(n_h):
+            ax[q, yy] = pair(q, yy, 0, 1 - x)
+        send(ax.at[q], axr.at[q], rs.at[q, 0], rr_.at[q, 0], *near_x)
         for xx in range(ratio):
-            sp[row, xx] = both[:, xx * cols:(xx + 1) * cols]
-            cp = copy(sp.at[row, xx], sr1.at[hh, xx], s1s.at[hh, xx], s1r.at[hh, xx], mate, c)
-            cp.start()
-            pending.append(cp)
-    for dh in order:
-        row = ((h + dh) % n_h) * 2 + k
-        both = dot3(fac(row), left_all, NT)
-        for xx in range(ratio):
-            sp[row, xx] = both[:, xx * cols:(xx + 1) * cols]
-    for i, (dh, dx) in enumerate(reversed(peers)):
-        row, xx = place(dh, dx, 0)
-        hh = row // 2
-        arrived(sr1.at[hh, xx], s1r.at[hh, xx])
-        sp2[hh, xx] = sp[row, xx] + sr1[hh, xx]
-        cp = copy(sp2.at[hh, xx], sr2.at[h, x], s2s.at[i], s2r.at[h, x], row, z * ratio + xx)
-        cp.start()
-        pending.append(cp)
-    arrived(sr1.at[h, x], s1r.at[h, x])
-    total = sp[r, x] + sr1[h, x]
-    for dh, dx in peers:
-        row, xx = place(dh, dx, 0)
-        hh = row // 2
-        arrived(sr2.at[hh, xx], s2r.at[hh, xx])
-        total = total + sr2[hh, xx]
-    st[...] = total
-    def swap(xx):
-        return copy(st.at[pl.ds(xx * cols, cols)], xr.at[x], xs.at[xx], xrs.at[x], z, r * ratio + xx)
-
-    for xx in range(ratio):
-        @pl.when((r != z) | (x != xx))
-        def _(xx=xx):
-            swap(xx).start()
-
-    @pl.when(r == z)
-    def _():
-        xr[x] = st[pl.ds(pl.multiple_of(x * cols, cols), cols)]
+            ay[q, xx] = pair(q, 1 - h, 1, xx)
+        send(ay.at[q], ayr.at[q], rs.at[q, 1], rr_.at[q, 1], *near_y)
+    for q in range(2):
+        arrived(axr.at[q], rr_.at[q, 0])
+        bx[q] = pair(q, 1 - h, 0, x) + axr[q, 1 - h]
+        send(bx.at[q], bxr.at[q], rs.at[q, 2], rr_.at[q, 2], *near_y)
+        arrived(ayr.at[q], rr_.at[q, 1])
+        by[q] = pair(q, h, 1, 1 - x) + ayr[q, 1 - x]
+        send(by.at[q], byr.at[q], rs.at[q, 3], rr_.at[q, 3], *near_x)
+
+    def swap(q, j):
+        return copy(
+            st.at[pl.ds(j * cols + q * fine, fine)], xr.at[x, pl.ds(q * fine, fine)],
+            xs.at[q, j], xrs.at[q, x], z, r * ratio + j,
+        )
+
+    for q in range(2):
+        low, high = slice(q * fine, (q + 1) * fine), slice(cols + q * fine, cols + (q + 1) * fine)
+        arrived(bxr.at[q], rr_.at[q, 2])
+        st[low] = pair(q, h, 0, x) + axr[q, h] + bxr[q]
+        arrived(byr.at[q], rr_.at[q, 3])
+        st[high] = pair(q, h, 1, x) + ayr[q, x] + byr[q]
+        for j in range(ratio):
+            @pl.when((r != z) | (x != j))
+            def _(q=q, j=j):
+                swap(q, j).start()
+
+        @pl.when(r == z)
+        def _(q=q, low=low):
+            xr[x, low] = st[pl.ds(pl.multiple_of(x * cols + q * fine, fine), fine)]
 
     lane = lax.broadcasted_iota(jnp.int32, (1, LANES), 1)
     group = LANES // own
@@ -363,46 +372,72 @@
             out = jnp.where(lane // own == j, row, out)
         return jnp.broadcast_to(out, (LANES, LANES))
 
-    col_energy = energy(z, x * group)
-    row_energy = [energy(r, xx * group).T for xx in range(ratio)]
-
-    for xx in range(ratio):
-        @pl.when((r != z) | (x != xx))
-        def _(xx=xx):
-            arrived(xr.at[xx], xrs.at[xx])
-
-        part = slice(xx * cols, (xx + 1) * cols)
-        new = -(st[part] + xr[xx].T) / (row_energy[xx] + col_energy)
-        tb[r, x, xx] = new.T
-        gather_start(tb, xx, ts, tr, us, ur)
-        t_ref[part] = new
-
-    for xx in range(ratio):
-        gather_relay(tb, xx, tr, us, ur)
-    for xx in range(ratio):
-        gather_end(tb, xx, ur)
-
-    def home(xx):
-        part = pl.ds(xx * cols, cols)
-        return copy(db.at[:, part], o_ref.at[:, part], ds_.at[xx], dr.at[xx], z, goal * ratio + x)
-
-    for xx in range(ratio):
+    col_energy = energy(z, x * group).T
+    bottom = [col_energy + energy(r, j * group) for j in range(ratio)]
+    top = [st[j * cols:(j + 1) * cols].T for j in range(ratio)]
+
+    def share(q):
+        part = slice(q * fine, (q + 1) * fine)
+        for xx in range(ratio):
+            @pl.when((r != z) | (x != xx))
+            def _(xx=xx):
+                arrived(xr.at[xx, pl.ds(q * fine, fine)], xrs.at[q, xx])
+
+        for j in range(ratio):
+            tb[r, x, j, part] = -(top[j][part] + xr[j, part]) / bottom[j][part]
+        for way, near in enumerate((near_x, near_y, (near_y[0], near_x[1]))):
+            send(tile(r, x, q), tile(r, x, q), ts.at[q, way], tr.at[q, way], *near)
+        relay(r, x, q, 0)
+
+    def tile(row, xx, q):
+        return tb.at[row, xx, :, pl.ds(q * fine, fine)]
+
+    def relay(row, xx, q, i):
+        send(tile(row, xx, q), tile(row, xx, q), us.at[q, i], ur.at[q, i], mate, c)
+
+    def collect(q):
+        for way, (row, xx) in enumerate(((r, 1 - x), (near_y[0], x), (near_y[0], 1 - x))):
+            arrived(tile(row, xx, q), tr.at[q, way])
+            relay(row, xx, q, 1 + way)
+
+    def finish(q):
+        other = near_y[0] + mate - r
+        for i, (row, xx) in enumerate(((mate, x), (mate, 1 - x), (other, x), (other, 1 - x))):
+            arrived(tile(row, xx, q), ur.at[q, i])
+
+    def home(q):
+        return copy(db.at[q], o_ref.at[q], ds_.at[q], dr.at[q], z, goal * ratio + x)
+
+    def density(q):
         d = None
+        part = slice(q * fine, (q + 1) * fine)
         for rr in range(n_row):
-            tile = jnp.concatenate([tb[rr, xx, i] for i in range(ratio)], axis=1)
-            term = dot3(halves(tile), fac(rr), NN)
+            block = jnp.concatenate([
+                jnp.concatenate([tb[rr, xx, j, part] for j in range(ratio)], axis=1) for xx in range(ratio)
+            ], axis=0)
+            term = dot3(halves(block), fac(rr), NN)
             d = term if d is None else d + term
-        part = slice(xx * cols, (xx + 1) * cols)
-        db[:LANES, part] = d[:, :LANES].T
-        db[LANES:, part] = d[:, LANES:].T
+        db[q, :LANES] = d[:, :LANES].T
+        db[q, LANES:] = d[:, LANES:].T
 
         @pl.when(~stays)
-        def _(xx=xx):
-            home(xx).start()
-
-    @pl.when(stays)
-    def _():
-        o_ref[...] = db[...]
+        def _():
+            home(q).start()
+
+        @pl.when(stays)
+        def _():
+            o_ref[q] = db[q]
+
+    share(0)
+    share(1)
+    collect(0)
+    finish(0)
+    density(0)
+    collect(1)
+    for j in range(ratio):
+        t_ref[j * cols:(j + 1) * cols] = tb[r, x, j].T
+    finish(1)
+    density(1)
 
     for cp in pending:
         cp.wait_send()
@@ -412,28 +447,32 @@
                 @pl.when(go)
                 def _(make=make):
                     make().wait_send()
-    for xx in range(ratio):
-        @pl.when((r != z) | (x != xx))
-        def _(xx=xx):
-            swap(xx).wait_send()
+    for q in range(2):
+        for j in range(ratio):
+            @pl.when((r != z) | (x != j))
+            def _(q=q, j=j):
+                swap(q, j).wait_send()
 
     @pl.when(~stays)
     def _():
-        for xx in range(ratio):
-            home(xx).wait_send()
-            home(xx).wait_recv()
+        for q in range(2):
+            home(q).wait_send()
+            home(q).wait_recv()
 
 
 def settle(new_ref, turned_ref, new_out, turned_out):
     new_out[...] = new_ref[...]
-    turned_out[...] = turned_ref[...]
+    low, high = turned_ref[0], turned_ref[1]
+    half = low.shape[1] // 2
+    turned_out[:, :2 * half] = jnp.concatenate([low[:, :half], high[:, :half]], axis=1)
+    turned_out[:, 2 * half:] = jnp.concatenate([low[:, half:], high[:, half:]], axis=1)
 
 
 def fits(mesh, rows, cols, own, width):
     n_row, n_col = mesh.shape["row"], mesh.shape["col"]
     ratio = n_col // n_row
     return (
-        n_col == ratio * n_row and n_col == SUB and ratio == 2 and n_row % 2 == 0
+        n_col == ratio * n_row and n_col == SUB and ratio == 2 and n_row == 4
         and rows == ratio * cols and cols == LANES
         and rows == n_col * own and LANES % own == 0 and own % (4 * SUB) == 0
         and 2 * width == 3 * LANES and 60 * rows * rows * n_row <= 64 * 2**20
@@ -451,15 +490,22 @@
     f32, bf16 = jnp.float32, jnp.bfloat16
     dma = pltpu.SemaphoreType.DMA
     vmem = pl.BlockSpec(memory_space=pltpu.VMEM)
+    fine = cols // 2
     new, turned = pl.pallas_call(
         functools.partial(kernel, n_row, ratio, own, width),
         out_shape=(
             jax.ShapeDtypeStruct((rows, cols), f32),
-            jax.ShapeDtypeStruct((width, rows), f32),
+            jax.ShapeDtypeStruct((2, width, cols), f32),
         ),
-        in_specs=[vmem] * 6,
+        in_specs=[pl.BlockSpec(memory_space=pltpu.HBM)] * 6,
         out_specs=(vmem, vmem),
         scratch_shapes=[
+            pltpu.VMEM(factors.shape, f32),
+            pltpu.VMEM((rows, cols), f32),
+            pltpu.VMEM((1, own), jnp.int32),
+            pltpu.VMEM((1, own), jnp.int32),
+            pltpu.VMEM((1,) + occ_energy.shape, f32),
+            pltpu.VMEM((1,) + vir_energy.shape, f32),
             pltpu.VMEM((n_col, deep, LANES), f32),
             pltpu.VMEM((n_col, SUB, LANES), f32),
             pltpu.VMEM((n_row, SUB, LANES), f32),
@@ -467,28 +513,38 @@
             pltpu.VMEM((n_row, rows, width), bf16),
             pltpu.VMEM((n_row, rows, width), bf16),
             pltpu.VMEM((n_row, ratio, cols, rows), f32),
-            pltpu.VMEM((n_row, ratio, rows, cols), f32),
-            pltpu.VMEM((n_h, ratio, rows, cols), f32),
-            pltpu.VMEM((n_h, ratio, rows, cols), f32),
-            pltpu.VMEM((n_h, ratio, rows, cols), f32),
+            pltpu.VMEM((2, n_h, ratio, ratio, fine, cols), f32),
+            pltpu.VMEM((2, n_h, ratio, ratio, fine, cols), f32),
+            pltpu.VMEM((2, n_h, ratio, ratio, fine, cols), f32),
+            pltpu.VMEM((2, n_h, fine, cols), f32),
+            pltpu.VMEM((2, n_h, fine, cols), f32),
+            pltpu.VMEM((2, ratio, fine, cols), f32),
+            pltpu.VMEM((2, ratio, fine, cols), f32),
+            pltpu.VMEM((2, fine, cols), f32),
+            pltpu.VMEM((2, fine, cols), f32),
+            pltpu.VMEM((2, fine, cols), f32),
+            pltpu.VMEM((2, fine, cols), f32),
             pltpu.VMEM((rows, cols), f32),
             pltpu.VMEM((ratio, cols, cols), f32),
             pltpu.VMEM((n_row, ratio, ratio, cols, cols), f32),
             pltpu.VMEM((ratio, cols, width), f32),
-            pltpu.VMEM((width, rows), f32),
+            pltpu.VMEM((2, width, cols), f32),
+            dma((6,)),
             dma((n_col - 1,)), dma((n_col,)),
             dma((n_col - 1,)), dma((n_col,)),
             dma((2, n_row, n_col + 1)), dma((n_row, n_col + 1)),
             dma((peers,)), dma((n_h, ratio)),
             dma((peers + 1,)), dma((n_h, ratio)),
-            dma((n_h, ratio)), dma((n_h, ratio)),
-            dma((peers,)), dma((n_h, ratio)),
-            dma((ratio,)), dma((ratio,)),
-            dma((ratio, peers)), dma((ratio, n_h, ratio)),
-            dma((ratio, peers + 1)), dma((ratio, n_h, ratio)),
-            dma((ratio,)), dma((ratio,)),
+            dma((2,)), dma((2,)),
+            dma((2, 4)), dma((2, 4)),
+            dma((2, ratio)), dma((2, ratio)),
+            dma((2, 3)), dma((2, 3)),
+            dma((2, 4)), dma((2, 4)),
+            dma((2,)), dma((2,)),
         ],
-        compiler_params=pltpu.CompilerParams(collective_id=0, has_side_effects=True),
+        compiler_params=pltpu.CompilerParams(
+            collective_id=0, has_side_effects=True
+        ),
     )(
         factors, amplitudes, occ_map[None, :], vir_map[None, :], occ_energy[None, :], vir_energy[None, :]
     )

time: 59.3 us -> 54.3 us (0.916)
  Pallas kernels: 58.5 us -> 53.5 us
    pallas_call x1, Pallas kernels: 56.8 us -> 51.7 us  [fused(): pl.pallas_call(functools.partial(kernel, n_row, ratio, own, width), out_s...]
where the time goes in v2:
time: 54.3 us; the launch traced here: 54.1 us
  Pallas kernels  53.5 us (99%)
  between operations  0.64 us (1%)
    pallas_call x1, Pallas kernels, fused(): pl.pallas_call(functools.partial(kernel, n_row, ratio, own, width), out_s...  51.7 us
    pallas_call x1, Pallas kernels, fused(): pl.pallas_call(settle, out_shape=(jax.ShapeDtypeStruct((rows, cols), f32)...  1.79 us

profile of v2, /device:TPU:1, one launch (start us, length us, event | category | flops | bytes accessed | tf_op | source)
XLA Modules:
  0.0 54.1 jit_solution(1646663158825131269)
XLA Ops:
  0.6 51.7 %shard_map.77 = (f32[256,128]{1,0:T(8,128)}, f32[2,192,128]{2,1,0:T(8,128)}) custom-call(f32[32,1536]{1,0:T(8,128)} %f_hbm.1, f32[256,128]{1,0:T(8,128)} %a_hbm.1, s32[1,32]{1,0:T(1,128)} %bitcast.6, s32[1,32]{1,0:T(1,128)} %bitcast.7, f32[1,128]{1,0:T(1,128)} %bitcast.8, f32[1,1024]{1,0:T(1,128)} %bitcast.5), custom_call_target="tpu_custom_call" | custom-call | tf_op jit(solution)/shard_map/pallas_call | solution.py:494
  52.3 1.8 %shard_map.78 = (f32[256,128]{1,0:T(8,128)}, f32[192,256]{1,0:T(8,128)}) custom-call(f32[256,128]{1,0:T(8,128)} %get-tuple-element.6.new_ref, f32[2,192,128]{2,1,0:T(8,128)} %get-tuple-element.7.turned_ref), custom_call_target="tpu_custom_call" | custom-call | tf_op jit(solution)/shard_map/pallas_call | solution.py:551

commit v3 on v2

--- a/solution.py
+++ b/solution.py
@@ -408,15 +408,21 @@
     def home(q):
         return copy(db.at[q], o_ref.at[q], ds_.at[q], dr.at[q], z, goal * ratio + x)
 
+    def terms(q, picked):
+        part = slice(q * fine, (q + 1) * fine)
+        d = None
+        for row in picked:
+            block = jnp.concatenate([
+                jnp.concatenate([tb[row, xx, j, part] for j in range(ratio)], axis=1) for xx in range(ratio)
+            ], axis=0)
+            term = dot3(halves(block), fac(row), NN)
+            d = term if d is None else d + term
+        return d
+
     def density(q):
-        d = None
-        part = slice(q * fine, (q + 1) * fine)
-        for rr in range(n_row):
-            block = jnp.concatenate([
-                jnp.concatenate([tb[rr, xx, j, part] for j in range(ratio)], axis=1) for xx in range(ratio)
-            ], axis=0)
-            term = dot3(halves(block), fac(rr), NN)
-            d = term if d is None else d + term
+        d = terms(q, (r, near_y[0]))
+        finish(q)
+        d = d + terms(q, (mate, near_y[0] + mate - r))
         db[q, :LANES] = d[:, :LANES].T
         db[q, LANES:] = d[:, LANES:].T
 
@@ -431,12 +437,10 @@
     share(0)
     share(1)
     collect(0)
-    finish(0)
     density(0)
     collect(1)
     for j in range(ratio):
         t_ref[j * cols:(j + 1) * cols] = tb[r, x, j].T
-    finish(1)
     density(1)
 
     for cp in pending:
@@ -494,8 +498,8 @@
     new, turned = pl.pallas_call(
         functools.partial(kernel, n_row, ratio, own, width),
         out_shape=(
-            jax.ShapeDtypeStruct((rows, cols), f32),
-            jax.ShapeDtypeStruct((2, width, cols), f32),
+            pltpu.VMEM((rows, cols), f32),
+            pltpu.VMEM((2, width, cols), f32),
         ),
         in_specs=[pl.BlockSpec(memory_space=pltpu.HBM)] * 6,
         out_specs=(vmem, vmem),
@@ -543,10 +547,12 @@
             dma((2,)), dma((2,)),
         ],
         compiler_params=pltpu.CompilerParams(
-            collective_id=0, has_side_effects=True
+            collective_id=0, has_side_effects=True, vmem_limit_bytes=32 * 2**20
         ),
     )(
-        factors, amplitudes, occ_map[None, :], vir_map[None, :], occ_energy[None, :], vir_energy[None, :]
+        *(pltpu.with_memory_space_constraint(v, pltpu.HBM) for v in (
+            factors, amplitudes, occ_map[None, :], vir_map[None, :], occ_energy[None, :], vir_energy[None, :]
+        ))
     )
     new, turned = pl.pallas_call(
         settle,
@@ -556,6 +562,7 @@
         ),
         in_specs=[vmem, vmem],
         out_specs=(vmem, vmem),
+        compiler_params=pltpu.CompilerParams(vmem_limit_bytes=4 * 2**20),
     )(new, turned)
     return new, turned.T
 

time: 54.3 us -> 52.4 us (0.965)
  Pallas kernels: 53.5 us -> 51.6 us
    pallas_call x1, Pallas kernels: 1.79 us -> 0.8 us  [fused(): pl.pallas_call(settle, out_shape=(jax.ShapeDtypeStruct((rows, cols), f32)...]
    pallas_call x1, Pallas kernels: 51.7 us -> 50.8 us  [fused(): pl.pallas_call(functools.partial(kernel, n_row, ratio, own, width), out_s...]
where the time goes in v3:
time: 52.4 us; the launch traced here: 52.2 us
  Pallas kernels  51.6 us (98%)
  between operations  0.64 us (1%)
    pallas_call x1, Pallas kernels, fused(): pl.pallas_call(functools.partial(kernel, n_row, ratio, own, width), out_s...  50.8 us

profile of v3, /device:TPU:1, one launch (start us, length us, event | category | flops | bytes accessed | tf_op | source)
XLA Modules:
  0.0 52.2 jit_solution(17709146745225897279)
XLA Ops:
  0.6 50.8 %shard_map.77 = (f32[256,128]{1,0:T(8,128)S(1)}, f32[2,192,128]{2,1,0:T(8,128)S(1)}) custom-call(f32[32,1536]{1,0:T(8,128)} %f_hbm.1, f32[256,128]{1,0:T(8,128)} %a_hbm.1, s32[1,32]{1,0:T(1,128)} %bitcast.6, s32[1,32]{1,0:T(1,128)} %bitcast.7, f32[1,128]{1,0:T(1,128)} %bitcast.8, f32[1,1024]{1,0:T(1,128)} %bitcast.5), custom_call_target="tpu_custom_call" | custom-call | tf_op jit(solution)/shard_map/pallas_call | solution.py:498
  51.4 0.8 %shard_map.78 = (f32[256,128]{1,0:T(8,128)}, f32[192,256]{1,0:T(8,128)}) custom-call(f32[256,128]{1,0:T(8,128)S(1)} %get-tuple-element.6.new_ref, f32[2,192,128]{2,1,0:T(8,128)S(1)} %get-tuple-element.7.turned_ref), custom_call_target="tpu_custom_call" | custom-call | tf_op jit(solution)/shard_map/pallas_call | solution.py:557
